TPU v7x, 128 devices: a whole 4x4x4 slice. The times are simulated.
128 devices in a mesh: row: 8 (over z_hi, y), col: 16 (over x, z_lo, core).
Axes of the slice: x: 4, y: 4, z: 4 (z_hi: 2, z_lo: 2; z = z_hi * 2 + z_lo), core: 2. Of those that a mesh axis runs over, the one named last changes fastest.
Arguments:
- features: bfloat16 [16, 8192, 128], P('col', 'row'), may hold values from 0.099609375 to 3
- relu_mask: int32 [16, 8192, 128], P('col', 'row'), may hold values 0 or 1
- tiles: bfloat16 [8, 16, 184, 256, 256], P('row', 'col'), may hold values from -0.25 to 0.25
- tile_rows: int32 [8, 16, 184], P('row', 'col'), may hold values from 0 to 63, as said below
- tile_cols: int32 [8, 16, 184], P('row', 'col'), may hold values from 0 to 31
- tile_count: int32 [8, 16], P('row', 'col'), may hold values from 23 to 184, as said below
- weight: bfloat16 [128, 128], replicated, may hold values from -0.5 to 0.5
- cotangent: bfloat16 [8, 16384, 128], P('row', 'col'), may hold values from -6 to 6
Outputs:
- out_pre: bfloat16 [8, 16384, 128], P('row', 'col')
- weight_grad: float32 [128, 128], replicated
- input_grad: bfloat16 [16, 8192, 128], P('col', 'row')
Inputs may be any that keep to these rules, and one draw needn't show every extreme that they name: `tile_rows`: within one panel pair the live and dead slots name distinct (block row, block column) pairs. `tile_count`: counts differ widely between panel pairs.
All inputs are finite; a program needn't handle non-finite values. No bound on the sum of `relu_mask` on one device may be relied on, other than what follows from the above.
Results may differ from a plain program's by a relative error of at most 0.022.
Values may be sent and summed in bfloat16 or wider, within the bound.
A program may use at most 192 MiB of HBM per device.

v0:
```python
import jax
import jax.numpy as jnp
from jax import lax
from jax.sharding import PartitionSpec as P


def slot_products(tile_vals, row_ids, col_ids, source, backward):
    tile_size = tile_vals.shape[1]
    feature_width = source.shape[1]
    if backward:
        blocks = source.reshape(-1, tile_size, feature_width)[row_ids]
        products = jnp.einsum("sij,sif->sjf", tile_vals, blocks, preferred_element_type=jnp.float32)
        target_ids = col_ids
    else:
        blocks = source.reshape(-1, tile_size, feature_width)[col_ids]
        products = jnp.einsum("sij,sjf->sif", tile_vals, blocks, preferred_element_type=jnp.float32)
        target_ids = row_ids
    return (products, target_ids)


def apply_tiles(tile_vals, row_ids, col_ids, live_count, source, backward, segments):
    feature_width = source.shape[1]
    slots = tile_vals.shape[0]
    products, target_ids = slot_products(tile_vals, row_ids, col_ids, source, backward)
    live_slots = jnp.arange(slots, dtype=jnp.int32) < live_count
    targets = jnp.arange(segments, dtype=jnp.int32)[:, None] == target_ids[None, :]
    selector = jnp.where(targets & live_slots[None, :], 1.0, 0.0).astype(jnp.float32)
    total = jnp.einsum(
        "rs,sif->rif",
        selector,
        products,
        precision=lax.Precision.HIGHEST,
        preferred_element_type=jnp.float32,
    )
    return total.reshape(-1, feature_width)


def body(features, relu_mask, tiles, tile_rows, tile_cols, tile_count, weight, cotangent):
    tile_size = tiles.shape[3]
    mask_rows = relu_mask[0]
    hidden = features[0] * mask_rows.astype(jnp.bfloat16)
    tile_vals = tiles[0, 0]
    row_ids = tile_rows[0, 0]
    col_ids = tile_cols[0, 0]
    live_count = tile_count[0, 0]
    own_rows = hidden.shape[0]
    row_blocks = own_rows * lax.axis_size("col") // tile_size
    col_blocks = own_rows * lax.axis_size("row") // tile_size
    feat_panel = lax.all_gather(hidden, "row", axis=0, tiled=True)
    forward_terms = apply_tiles(
        tile_vals, row_ids, col_ids, live_count, feat_panel, False, row_blocks
    )
    forward_terms = lax.optimization_barrier(forward_terms.astype(jnp.bfloat16)).astype(jnp.float32)
    aggregate = lax.psum_scatter(
        forward_terms.astype(jnp.bfloat16), "col", scatter_dimension=0, tiled=True
    )
    out_pre = jnp.dot(aggregate, weight, preferred_element_type=jnp.float32).astype(jnp.bfloat16)
    cot_rows = cotangent[0]
    weight_term = lax.dot_general(
        aggregate, cot_rows, (((0,), (0,)), ((), ())), preferred_element_type=jnp.float32
    )
    grad_scale = 1.0 / jnp.sqrt(jnp.float32(own_rows * lax.axis_size("row") * lax.axis_size("col")))
    weight_grad = lax.psum(weight_term, ("row", "col")) * grad_scale
    grad_rows = lax.dot_general(
        cot_rows, weight, (((1,), (1,)), ((), ())), preferred_element_type=jnp.float32
    )
    grad_rows = lax.all_gather(grad_rows.astype(jnp.bfloat16), "col", axis=0, tiled=True)
    back_terms = apply_tiles(tile_vals, row_ids, col_ids, live_count, grad_rows, True, col_blocks)
    back_terms = lax.optimization_barrier(back_terms.astype(jnp.bfloat16)).astype(jnp.float32)
    summed = lax.psum_scatter(
        back_terms.astype(jnp.bfloat16), "row", scatter_dimension=0, tiled=True
    ).astype(jnp.float32)
    input_grad = (summed * mask_rows.astype(jnp.float32)).astype(jnp.bfloat16)
    return (out_pre[None], weight_grad, input_grad[None])


def solution(mesh):
    placed = (
        P("col", "row", None),
        P("col", "row", None),
        P("row", "col", None, None, None),
        P("row", "col", None),
        P("row", "col", None),
        P("row", "col"),
        P(),
        P("row", "col", None),
    )
    return jax.shard_map(
        body,
        mesh=mesh,
        in_specs=placed,
        out_specs=(P("row", "col", None), P(), P("col", "row", None)),
        check_vma=False,
    )
```

profile of v0, /device:TPU:1, one launch (start us, length us, event | category | flops | bytes accessed | tf_op | source)
XLA Modules:
  0.0 451.3 jit_solution(6644754055595961643)
XLA Ops:
  7.2 0.0 all-gather.6.cloned.1.call-start
  7.2 1.9 convert_multiply_fusion
  9.1 0.0 all-gather.6.cloned.1.call-update
  9.1 0.0 all-gather.4.cloned.1.call-start
  9.2 1.7 convolution_convert_fusion
  10.9 0.0 all-gather.4.cloned.1.call-update
  10.9 0.0 reduce-scatter.3.cloned.1.call-start
  11.6 0.7 compare_select_fusion.1
  12.3 55.5 %all-gather.6.cloned.1.call-done = bf16[1,8192,128]{2,1,0:T(8,128)(2,1)} async-done(((bf16[1,1024,128]{2,1,0:T(8,128)(2,1)}), bf16[1,8192,128]{2,1,0:T(8,128)(2,1)}) %all-gather.6.cloned.1.call-update) | async-done | bytes 2097168 | tf_op jit(solution)/shard_map/all_gather | solution.py:49
  67.9 9.6 %gather_fusion = bf16[184,256,128]{2,1,0:T(8,128)(2,1)} fusion(bf16[32,256,128]{2,1,0:T(8,128)(2,1)} %bitcast.56, s32[1024]{0:T(1024)S(1)} %pad_clamp_fusion.1), kind=kCustom, calls=%fused_computation | custom fusion | bytes 24117984 | tf_op jit(solution)/shard_map/gather | solution.py:15
  77.5 21.6 %fusion.6 = f32[184,128,256]{2,1,0:T(8,128)} fusion(bf16[184,256,128]{2,1,0:T(8,128)(2,1)} %gather_fusion, bf16[1,1,184,256,256]{4,3,2,1,0:T(8,128)(2,1)} %param.10), kind=kOutput, calls=%fused_computation.8 | convolution fusion | flops 3087007744 | bytes 60293120 | tf_op jit(solution)/shard_map/sij,sjf->sif/dot_general | solution.py:16
  99.1 24.6 %copy.13 = f32[184,128,256]{1,0,2:T(8,128)} copy(f32[184,128,256]{2,1,0:T(8,128)} %fusion.6) | data formatting | bytes 48234496 | tf_op jit(solution)/shard_map/sij,sjf->sif/dot_general | solution.py:16
  123.7 20.8 %fusion.8 = bf16[64,256,128]{2,0,1:T(8,128)(2,1)S(1)} fusion(f32[184,128,256]{1,0,2:T(8,128)} %copy.13, s32[184]{0:T(256)S(1)} %bitcast.60, pred[184]{0:T(512)(128)(4,1)S(1)} %iota_compare_fusion.2), kind=kOutput, calls=%fused_computation.10 | convolution fusion | flops 4632644096 | bytes 28312472 | tf_op jit(solution)/shard_map/rs,sif->rif/dot_general | solution.py:28
  144.5 4.7 %copy.11 = bf16[64,256,128]{2,1,0:T(8,128)(2,1)} copy(bf16[64,256,128]{2,0,1:T(8,128)(2,1)S(1)} %fusion.8) | data formatting | bytes 8388608 | tf_op jit(solution)/shard_map/convert_element_type | solution.py:53
  149.1 0.0 reduce-scatter.3.cloned.1.call-update
  149.2 0.0 reduce-scatter.5.cloned.1.call-start
  149.2 0.0 all-gather.4.cloned.1.call-done
  149.3 10.3 %gather_fusion.1 = bf16[184,256,128]{2,1,0:T(8,128)(2,1)} fusion(bf16[64,256,128]{2,1,0:T(8,128)(2,1)} %bitcast.57, s32[1024]{0:T(1024)S(1)} %pad_clamp_fusion), kind=kCustom, calls=%fused_computation.1 | custom fusion | bytes 24117984 | tf_op jit(solution)/shard_map/gather | solution.py:11
  159.5 22.0 %fusion.4 = f32[184,128,256]{2,1,0:T(8,128)} fusion(bf16[184,256,128]{2,1,0:T(8,128)(2,1)} %gather_fusion.1, bf16[1,1,184,256,256]{4,3,2,1,0:T(8,128)(2,1)} %param.10), kind=kOutput, calls=%fused_computation.6 | convolution fusion | flops 3087007744 | bytes 60293120 | tf_op jit(solution)/shard_map/sij,sif->sjf/dot_general | solution.py:12
  181.6 24.6 %copy.14 = f32[184,128,256]{1,0,2:T(8,128)} copy(f32[184,128,256]{2,1,0:T(8,128)} %fusion.4) | data formatting | bytes 48234496 | tf_op jit(solution)/shard_map/sij,sif->sjf/dot_general | solution.py:12
  206.2 17.1 %fusion.11 = bf16[32,256,128]{2,0,1:T(8,128)(2,1)S(1)} fusion(f32[184,128,256]{1,0,2:T(8,128)} %copy.14, s32[184]{0:T(256)S(1)} %bitcast.61, pred[184]{0:T(512)(128)(4,1)S(1)} %iota_compare_fusion.2), kind=kOutput, calls=%fused_computation.11 | convolution fusion | flops 2316322048 | bytes 26215320 | tf_op jit(solution)/shard_map/rs,sif->rif/dot_general | solution.py:28
  223.3 2.1 copy.12
  225.4 0.0 reduce-scatter.5.cloned.1.call-update
  225.4 0.0 all-reduce.2.cloned.1.call-start
  225.5 0.0 reduce-scatter.3.cloned.1.call-done
  225.5 1.9 fusion.18
  227.3 0.0 all-reduce.2.cloned.1.call-update
  227.4 1.9 fusion.14
  229.2 70.5 %reduce-scatter.5.cloned.1.call-done = bf16[1024,128]{1,0:T(8,128)(2,1)} async-done(((bf16[8192,128]{1,0:T(8,128)(2,1)}), bf16[1024,128]{1,0:T(8,128)(2,1)}) %reduce-scatter.5.cloned.1.call-update) | async-done | bytes 262160 | tf_op jit(solution)/shard_map/reduce_scatter | solution.py:70
  299.7 1.7 fusion.16
  301.5 141.9 %all-reduce.2.cloned.1.call-done = f32[128,128]{1,0:T(8,128)} async-done(((f32[128,128]{1,0:T(8,128)}), f32[128,128]{1,0:T(8,128)}) %all-reduce.2.cloned.1.call-update) | async-done | bytes 65552 | tf_op jit(solution)/shard_map/psum | solution.py:63
  443.3 1.5 broadcast_multiply_fusion
  (14 shorter events, 0.0 us)
Async XLA Ops:
  7.2 2.0 copy-start
  7.2 60.7 %all-gather.6.cloned.1.call-start = ((), (), s32[]{:S(2)}) async-start(), calls=%async_computation.6 | async-start | bytes 2359296 | tf_op jit(solution)/shard_map/all_gather | solution.py:49
  9.1 140.1 %all-gather.4.cloned.1.call-start = ((), (), s32[]{:S(2)}) async-start(), calls=%async_computation.4 | async-start | bytes 4456448 | tf_op jit(solution)/shard_map/all_gather | solution.py:67
  10.9 214.6 %reduce-scatter.3.cloned.1.call-start = ((), (), s32[]{:S(2)}) async-start(), calls=%async_computation.2 | async-start | bytes 4456448 | tf_op jit(solution)/shard_map/reduce_scatter | solution.py:54
  99.1 24.6 %copy-start.3 = (s32[1,1,184]{2,1,0:T(1,128)S(1)}, s32[1,1,184]{2,1,0:T(1,128)}, u32[]{:S(2)}) copy-start(s32[1,1,184]{2,1,0:T(1,128)} %param.11) | copy-start | bytes 2212
  149.2 150.6 %reduce-scatter.5.cloned.1.call-start = ((), (), s32[]{:S(2)}) async-start(), calls=%async_computation.5 | async-start | bytes 2359296 | tf_op jit(solution)/shard_map/reduce_scatter | solution.py:70
  181.6 24.6 %copy-start.4 = (s32[1,1,184]{2,1,0:T(1,128)S(1)}, s32[1,1,184]{2,1,0:T(1,128)}, u32[]{:S(2)}) copy-start(s32[1,1,184]{2,1,0:T(1,128)} %param.12) | copy-start | bytes 2212
  206.2 21.2 %copy-start.2 = (bf16[128,128]{1,0:T(8,128)(2,1)S(1)}, bf16[128,128]{1,0:T(8,128)(2,1)}, u32[]{:S(2)}) copy-start(bf16[128,128]{1,0:T(8,128)(2,1)} %param.14) | copy-start | bytes 98308
  206.2 93.6 %copy-start.1 = (s32[1,1024,128]{2,1,0:T(8,128)S(1)}, s32[1,1024,128]{2,1,0:T(8,128)}, u32[]{:S(2)}) copy-start(s32[1,1024,128]{2,1,0:T(8,128)} %param.9) | copy-start | bytes 1572868
  225.4 217.9 %all-reduce.2.cloned.1.call-start = ((), (), s32[]{:S(2)}) async-start(), calls=%async_computation.3 | async-start | bytes 131072 | tf_op jit(solution)/shard_map/psum | solution.py:63
Sparse Core Ops, SparseCore 0:
  10.9 56.9 all-gather.5
  70.1 37.8 all-gather.3
  149.3 63.8 reduce-scatter.2
  225.5 74.1 reduce-scatter.4
  305.6 137.6 all-reduce.1
where the time goes:
time: 452 us; the launch traced here: 451 us
  waiting for transfers between devices  268 us (59%)
  matrix products  86.9 us (19%)
  local copies, waits for them, and re-layouts  75.9 us (17%)
  between operations  14.5 us (3%)
  other arithmetic  5.8 us (1%)
    psum x1, waiting for transfers between devices, body(): weight_grad = lax.psum(weight_term, ('row', 'col')) * grad_scale  142 us
    reduce_scatter x1, waiting for transfers between devices, body(): lax.psum_scatter(back_terms.astype(jnp.bfloat16), 'row', scatter_dimensio...  70.5 us
    all_gather x1, waiting for transfers between devices, body(): feat_panel = lax.all_gather(hidden, 'row', axis=0, tiled=True)  55.5 us
    dot_general x2, matrix products, apply_tiles(): jnp.einsum('rs,sif->rif', selector, products, precision=lax.Precision.HIG...  37.9 us
    dot_general x1, local copies, waits for them, and re-layouts, slot_products(): jnp.einsum('sij,sif->sjf', tile_vals, blocks, preferred_element_type=jnp....  24.6 us
    dot_general x1, local copies, waits for them, and re-layouts, slot_products(): jnp.einsum('sij,sjf->sif', tile_vals, blocks, preferred_element_type=jnp....  24.6 us
    dot_general x1, matrix products, slot_products(): jnp.einsum('sij,sif->sjf', tile_vals, blocks, preferred_element_type=jnp....  22 us
    dot_general x1, matrix products, slot_products(): jnp.einsum('sij,sjf->sif', tile_vals, blocks, preferred_element_type=jnp....  21.6 us
  transfers between devices with their start and end apart: 5, of which 3 were waited for; matrix products, arithmetic and copies ran while one was open for 37% of the time, Pallas kernels for 0%

commit v1 on v0

v1 whole, which is shorter than its diff:
```python
import functools

import jax
import jax.numpy as jnp
from jax import lax
from jax.experimental import pallas as pl
from jax.experimental.pallas import tpu as pltpu
from jax.sharding import PartitionSpec as P

MESH = pl.DeviceIdType.MESH
F32 = jnp.float32
BF16 = jnp.bfloat16
UNROLL = 4
N_COPIES = 96


def plan(tile_rows, tile_cols, tile_count, row_blocks, col_blocks):
    slots = tile_rows.shape[0]
    ids = jnp.arange(slots, dtype=jnp.int32)
    dead = ids >= tile_count

    def one(target, source, targets, sources):
        key = target * sources + source + jnp.where(dead, targets * sources, 0)
        rank = jnp.sum((key[None, :] < key[:, None]).astype(jnp.int32), axis=1)
        hit = rank[:, None] == ids[None, :]

        def permute(values):
            return jnp.sum(jnp.where(hit, values[:, None], 0), axis=0)

        goal = jnp.where(dead, targets, target)
        same = (goal[:, None] == goal[None, :]) & (rank[None, :] < rank[:, None])
        head = 1 - jnp.max(same.astype(jnp.int32), axis=1)
        blocks = jnp.arange(targets, dtype=jnp.int32)
        upto = jnp.sum((goal[None, :] <= blocks[:, None]).astype(jnp.int32), axis=1)
        count = jnp.sum((goal[None, :] == blocks[:, None]).astype(jnp.int32), axis=1)
        last = jnp.maximum(upto - 1, 0)
        return [permute(ids), permute(source), permute(head), last, jnp.minimum(count, 1)]

    parts = one(tile_rows, tile_cols, row_blocks, col_blocks)
    parts += one(tile_cols, tile_rows, col_blocks, row_blocks)
    return jnp.concatenate(parts)


def kernel(
    slots, row_blocks, col_blocks, per, scale,
    tab, feat_hbm, mask_hbm, tiles_hbm, w_hbm, cot_hbm,
    out_ref, wg_ref, ig_ref,
    feat_v, mask_v, w_v, cot_v, tiles_v,
    hid, grd, prods, fpart, bpart, sib, xsum,
    ra, rb, fr, fl, zs, zb,
    acc_f, acc_b, agg, tb, ac, ax, ay, az, ws,
    send_sem, recv_sem, local_sem,
):
    r = lax.axis_index("row")
    c = lax.axis_index("col")
    zh, y = r // 4, lax.rem(r, 4)
    x, zl, core = c // 4, lax.rem(c // 2, 2), lax.rem(c, 2)

    def col_of(xx, zz, kk):
        return xx * 4 + zz * 2 + kk

    def at_x(step):
        return lax.rem(x + step, 4)

    def at_y(step):
        return lax.rem(y + step, 4)

    def x_dev(step):
        return {"row": r, "col": col_of(at_x(step), zl, core)}

    def y_dev(step):
        return {"row": zh * 4 + at_y(step), "col": c}

    sib_dev = {"row": r, "col": col_of(x, zl, 1 - core)}
    zl_dev = {"row": r, "col": col_of(x, 1 - zl, core)}
    zh_dev = {"row": (1 - zh) * 4 + y, "col": c}
    zz_dev = {"row": (1 - zh) * 4 + y, "col": col_of(x, 1 - zl, core)}
    right, left, up, down = x_dev(1), x_dev(3), y_dev(1), y_dev(3)
    peers = [sib_dev, right, left, x_dev(2), up, down, y_dev(2), zl_dev, zh_dev, zz_dev]

    loads = [(feat_hbm, feat_v), (mask_hbm, mask_v), (w_hbm, w_v), (cot_hbm, cot_v), (tiles_hbm, tiles_v)]
    loads = [pltpu.make_async_copy(s, d, local_sem.at[i]) for i, (s, d) in enumerate(loads)]
    for load in loads:
        load.start()

    barrier = pltpu.get_barrier_semaphore()
    for peer in peers:
        pl.semaphore_signal(barrier, inc=1, device_id=peer, device_id_type=MESH)

    made = []

    def send(src, dst, dev):
        i = len(made)
        copy = pltpu.make_async_remote_copy(
            src_ref=src, dst_ref=dst, send_sem=send_sem.at[i], recv_sem=recv_sem.at[i],
            device_id=dev, device_id_type=MESH,
        )
        copy.start()
        made.append(copy)
        return copy

    half = per // 2

    def col_shard(xx, zz, kk, first=0, size=per):
        return grd.at[pl.ds(col_of(xx, zz, kk) * per + first, size)]

    def row_shard(zz, yy, first=0, size=per):
        return hid.at[pl.ds((zz * 4 + yy) * per + first, size)]

    def share(ref, dev):
        return send(ref, ref, dev)

    loads[2].wait()
    loads[3].wait()
    for j in range(per):
        block = lax.dot_general(
            w_v[...], cot_v[j * 256 : (j + 1) * 256], (((1,), (1,)), ((), ())), preferred_element_type=F32
        )
        grd[c * per + j] = block.astype(BF16)
    loads[0].wait()
    loads[1].wait()
    for j in range(per):
        rows = slice(j * 256, (j + 1) * 256)
        hid[r * per + j] = feat_v[rows] * mask_v[rows].astype(F32).astype(BF16)

    pl.semaphore_wait(barrier, len(peers))

    c_r = share(col_shard(x, zl, core), right)
    c_l = share(col_shard(x, zl, core), left)
    r_u = share(row_shard(zh, y), up)
    r_d = share(row_shard(zh, y), down)
    r_z = share(row_shard(zh, y), zh_dev)
    c_z = share(col_shard(x, zl, core), zl_dev)
    c_s = [share(col_shard(x, zl, core), sib_dev)]

    c_z.wait_recv()
    cz_r = share(col_shard(x, 1 - zl, core), right)
    cz_l = share(col_shard(x, 1 - zl, core), left)
    c_s.append(share(col_shard(x, 1 - zl, core), sib_dev))
    r_z.wait_recv()
    rz_u = share(row_shard(1 - zh, y), up)
    rz_d = share(row_shard(1 - zh, y), down)

    def relay_x(from_left, from_right, zz):
        from_left.wait_recv()
        a = share(col_shard(at_x(3), zz, core, 0, half), right)
        c_s.append(share(col_shard(at_x(3), zz, core), sib_dev))
        from_right.wait_recv()
        b = share(col_shard(at_x(1), zz, core, half, half), left)
        c_s.append(share(col_shard(at_x(1), zz, core), sib_dev))
        return a, b

    def relay_y(from_down, from_up, zz):
        from_down.wait_recv()
        a = share(row_shard(zz, at_y(3), 0, half), up)
        from_up.wait_recv()
        b = share(row_shard(zz, at_y(1), half, half), down)
        return a, b

    ya, yb = relay_y(r_u, r_d, zh)
    xa, xb = relay_x(c_r, c_l, zl)
    yza, yzb = relay_y(rz_u, rz_d, 1 - zh)
    xza, xzb = relay_x(cz_r, cz_l, 1 - zl)
    for copy in (ya, yb, yza, yzb):
        copy.wait_recv()
    loads[4].wait()

    o_f = 0
    o_b = 3 * slots + 2 * row_blocks

    def fwd_range(lo, hi):
        @pl.loop(lo, hi)
        def _(g):
            acc = acc_f[...]
            for u in range(UNROLL):
                p = g * UNROLL + u
                prod = jnp.dot(
                    tiles_v[tab[o_f + p]], hid[tab[o_f + slots + p]], preferred_element_type=F32
                )
                acc = jnp.where(tab[o_f + 2 * slots + p] == 1, 0.0, acc) + prod
                prods[p] = acc.astype(BF16)
            acc_f[...] = acc

    def bwd_range(lo, hi):
        @pl.loop(lo, hi)
        def _(g):
            acc = acc_b[...]
            for u in range(UNROLL):
                p = g * UNROLL + u
                prod = jnp.dot(
                    grd[tab[o_b + slots + p]], tiles_v[tab[o_b + p]], preferred_element_type=F32
                )
                acc = jnp.where(tab[o_b + 2 * slots + p] == 1, 0.0, acc) + prod
                prods[p, 0:128, :] = acc[:, 0:128].astype(BF16)
                prods[p, 128:256, :] = acc[:, 128:256].astype(BF16)
            acc_b[...] = acc

    groups = slots // UNROLL
    acc_f[...] = jnp.zeros_like(acc_f)
    acc_b[...] = jnp.zeros_like(acc_b)

    fwd_range(0, groups // 2)
    for copy, zz, sx, first in ((xa, zl, 3, 0), (xb, zl, 1, half)):
        copy.wait_recv()
        c_s.append(share(col_shard(at_x(2), zz, core, first, half), sib_dev))
    fwd_range(groups // 2, groups)
    for copy, zz, first in ((xza, 1 - zl, 0), (xzb, 1 - zl, half)):
        copy.wait_recv()
        c_s.append(share(col_shard(at_x(2), zz, core, first, half), sib_dev))

    def take(dst, block, offset, targets):
        i = offset + 3 * slots + block
        value = prods[tab[i]]
        dst[block] = jnp.where(tab[i + targets] == 1, value, jnp.zeros_like(value))

    zs_of = (1 - zl, zl)

    def fill(kk):
        @pl.loop(0, row_blocks // 2)
        def _(m):
            take(fpart, (m // per) * 2 * per + kk * per + lax.rem(m, per), o_f, row_blocks)

    fill(1 - core)
    sibs = {}
    for dz in range(2):
        for dx in (2, 1, 3, 0):
            src = fpart.at[pl.ds(col_of(at_x(dx), zs_of[dz], 1 - core) * per, per)]
            sibs[dz, dx] = send(src, sib.at[dz, dx], sib_dev)
    fill(core)

    def with_sibling(dz, dx):
        sibs[dz, dx].wait_recv()
        base = col_of(at_x(dx), zs_of[dz], core) * per

        @pl.loop(0, per)
        def _(j):
            xsum[dz, dx, j] = (fpart[base + j].astype(F32) + sib[dz, dx, j].astype(F32)).astype(BF16)

    def add_into(dst, first, other):
        @pl.loop(0, half)
        def _(j):
            dst[first + j] = (dst[first + j].astype(F32) + other[j].astype(F32)).astype(BF16)

    def ring_sum(k, part, prepare, ahead, behind, z_dev, finish):
        a, b = (0, half), (half, half)

        def piece(dz, d, ab):
            return part(dz, d).at[pl.ds(ab[0], ab[1])]

        first, second = {}, {}

        def far(dz):
            prepare(dz, 2)
            first[dz] = (
                send(piece(dz, 2, a), ra.at[k, dz], ahead),
                send(piece(dz, 2, b), rb.at[k, dz], behind),
            )

        def near(dz):
            prepare(dz, 1)
            prepare(dz, 3)
            second[dz] = [
                send(piece(dz, 1, b), fr.at[k, dz, pl.ds(half, half)], ahead),
                send(piece(dz, 3, a), fl.at[k, dz, pl.ds(0, half)], behind),
            ]

        def relay(dz):
            first[dz][0].wait_recv()
            add_into(part(dz, 1), 0, ra.at[k, dz])
            second[dz].append(send(piece(dz, 1, a), fr.at[k, dz, pl.ds(0, half)], ahead))
            first[dz][1].wait_recv()
            add_into(part(dz, 3), half, rb.at[k, dz])
            second[dz].append(send(piece(dz, 3, b), fl.at[k, dz, pl.ds(half, half)], behind))

        def total(dz, j):
            return part(dz, 0)[j].astype(F32) + fr[k, dz, j].astype(F32) + fl[k, dz, j].astype(F32)

        far(0)
        near(0)
        far(1)
        yield
        relay(0)
        near(1)
        yield
        relay(1)
        prepare(0, 0)
        prepare(1, 0)
        yield
        for copy in second[0]:
            copy.wait_recv()

        @pl.loop(0, per)
        def _(j):
            zs[k, j] = total(0, j).astype(BF16)

        last = send(zs.at[k], zb.at[k], z_dev)
        yield
        for copy in second[1]:
            copy.wait_recv()
        last.wait_recv()
        for j in range(per):
            finish(j, total(1, j) + zb[k, j].astype(F32))

    def finish_f(j, value):
        agg[j * 256 : (j + 1) * 256] = value.astype(BF16)

    def finish_b(j, value):
        for h in range(2):
            rows = slice(j * 256 + h * 128, j * 256 + h * 128 + 128)
            ig_ref[rows] = (value[h * 128 : (h + 1) * 128].T * mask_v[rows].astype(F32)).astype(BF16)

    sum_f = ring_sum(0, lambda dz, d: xsum.at[dz, d], with_sibling, right, left, zl_dev, finish_f)

    zh_of = (1 - zh, zh)
    sum_b = ring_sum(
        1,
        lambda dz, d: bpart.at[pl.ds((zh_of[dz] * 4 + at_y(d)) * per, per)],
        lambda dz, d: None,
        up, down, zh_dev, finish_b,
    )

    for copy in c_s:
        copy.wait_recv()
    bounds = [groups * i // 4 for i in range(5)]
    bwd_range(bounds[0], bounds[1])
    next(sum_f)
    bwd_range(bounds[1], bounds[2])
    next(sum_f)
    bwd_range(bounds[2], bounds[3])
    next(sum_f)
    bwd_range(bounds[3], bounds[4])

    @pl.loop(0, col_blocks)
    def _(m):
        take(bpart, m, o_b, col_blocks)

    next(sum_b)
    next(sum_f)
    next(sum_b)
    next(sum_f, None)

    out_ref[...] = jnp.dot(agg[...], w_v[...], preferred_element_type=F32).astype(BF16)
    tb[...] = lax.dot_general(agg[...], cot_v[...], (((0,), (0,)), ((), ())), preferred_element_type=F32)
    rows = tb.shape[0] // 2
    to_sib = send(tb.at[pl.ds((1 - core) * rows, rows)], ac, sib_dev)
    next(sum_b)
    to_sib.wait_recv()
    ax[x] = tb[pl.ds(core * rows, rows)] + ac[...]
    ring = [send(ax.at[x], ax.at[x], x_dev(s)) for s in (1, 3, 2)]
    next(sum_b)
    for copy in ring:
        copy.wait_recv()
    ay[y] = (ax[0] + ax[1]) + (ax[2] + ax[3])
    ring = [send(ay.at[y], ay.at[y], y_dev(s)) for s in (1, 3, 2)]
    next(sum_b, None)
    for copy in ring:
        copy.wait_recv()
    z = zh * 2 + zl
    az[z] = (ay[0] + ay[1]) + (ay[2] + ay[3])
    ring = [send(az.at[z], az.at[z], dev) for dev in (zl_dev, zh_dev, zz_dev)]
    for copy in ring:
        copy.wait_recv()
    ws[core] = ((az[0] + az[1]) + (az[2] + az[3])) * scale
    last = share(ws.at[core], sib_dev)
    last.wait_recv()
    wg_ref[0:rows] = ws[0]
    wg_ref[rows : 2 * rows] = ws[1]

    for copy in made:
        copy.wait_send()


def body(features, relu_mask, tiles, tile_rows, tile_cols, tile_count, weight, cotangent):
    slots, tile = tiles.shape[2], tiles.shape[3]
    own, width = features.shape[1:]
    per = own // tile
    row_blocks, col_blocks = per * lax.axis_size("col"), per * lax.axis_size("row")
    half = per // 2
    scale = float((own * lax.axis_size("row") * lax.axis_size("col")) ** -0.5)
    table = plan(tile_rows[0, 0], tile_cols[0, 0], tile_count[0, 0], row_blocks, col_blocks)
    block = (tile, width)
    v = pltpu.VMEM
    anywhere = pl.BlockSpec(memory_space=pl.ANY)
    in_vmem = pl.BlockSpec(memory_space=pltpu.VMEM)
    out_pre, weight_grad, input_grad = pl.pallas_call(
        functools.partial(kernel, slots, row_blocks, col_blocks, per, scale),
        out_shape=(
            jax.ShapeDtypeStruct((own, width), BF16),
            jax.ShapeDtypeStruct((width, width), F32),
            jax.ShapeDtypeStruct((own, width), BF16),
        ),
        in_specs=[pl.BlockSpec(memory_space=pltpu.SMEM)] + [anywhere] * 5,
        out_specs=(in_vmem,) * 3,
        scratch_shapes=[
            v((own, width), BF16),
            v((own, width), jnp.int32),
            v((width, width), BF16),
            v((own, width), BF16),
            v((slots, tile, tile), BF16),
            v((col_blocks,) + block, BF16),
            v((row_blocks, width, tile), BF16),
            v((slots,) + block, BF16),
            v((row_blocks,) + block, BF16),
            v((col_blocks,) + block, BF16),
            v((2, 4, per) + block, BF16),
            v((2, 4, per) + block, BF16),
            v((2, 2, half) + block, BF16),
            v((2, 2, half) + block, BF16),
            v((2, 2, per) + block, BF16),
            v((2, 2, per) + block, BF16),
            v((2, per) + block, BF16),
            v((2, per) + block, BF16),
            v(block, F32),
            v((width, tile), F32),
            v((own, width), BF16),
            v((width, width), F32),
            v((width // 2, width), F32),
            v((4, width // 2, width), F32),
            v((4, width // 2, width), F32),
            v((4, width // 2, width), F32),
            v((2, width // 2, width), F32),
            pltpu.SemaphoreType.DMA((N_COPIES,)),
            pltpu.SemaphoreType.DMA((N_COPIES,)),
            pltpu.SemaphoreType.DMA((5,)),
        ],
        compiler_params=pltpu.CompilerParams(
            collective_id=0, has_side_effects=True, vmem_limit_bytes=67043328
        ),
        name="layer",
    )(table, features[0], relu_mask[0], tiles[0, 0], weight, cotangent[0])
    return out_pre[None], weight_grad, input_grad[None]


def solution(mesh):
    placed = (
        P("col", "row", None),
        P("col", "row", None),
        P("row", "col", None, None, None),
        P("row", "col", None),
        P("row", "col", None),
        P("row", "col"),
        P(),
        P("row", "col", None),
    )
    return jax.shard_map(
        body,
        mesh=mesh,
        in_specs=placed,
        out_specs=(P("row", "col", None), P(), P("col", "row", None)),
        check_vma=False,
    )
```

time: 452 us -> 108 us (0.24)
  waiting for transfers between devices: 268 us -> 0 us
  Pallas kernels: 0 us -> 97.7 us
  matrix products: 86.9 us -> 0 us
  local copies, waits for them, and re-layouts: 75.9 us -> 5.5 us
  between operations: 14.5 us -> 1.34 us
    psum x1 -> x0, waiting for transfers between devices: 142 us -> none  [body(): weight_grad = lax.psum(weight_term, ('row', 'col')) * grad_scale]
    pallas_call x0 -> x1, Pallas kernels: none -> 97.7 us  [body(): pl.pallas_call(functools.partial(kernel, slots, row_blocks, col_blocks, p...]
    dot_general x7 -> x0, matrix products: 86.9 us -> none  [the longest x2 37.9 us: apply_tiles(): jnp.einsum('rs,sif->rif', selector, products, precision=lax.Precision.HIG...]
    reduce_scatter x2 -> x0, waiting for transfers between devices: 70.5 us -> none  [the longest x1 70.5 us: body(): lax.psum_scatter(back_terms.astype(jnp.bfloat16), 'row', scatter_dimensio...]
    all_gather x2 -> x0, waiting for transfers between devices: 55.6 us -> none  [the longest x1 55.5 us: body(): feat_panel = lax.all_gather(hidden, 'row', axis=0, tiled=True)]
    dot_general x2 -> x0, local copies, waits for them, and re-layouts: 49.2 us -> none  [the longest x1 24.6 us: slot_products(): jnp.einsum('sij,sif->sjf', tile_vals, blocks, preferred_element_type=jnp....]
    gather x2 -> x0, local copies, waits for them, and re-layouts: 19.9 us -> none  [the longest x1 10.3 us: slot_products(): blocks = source.reshape(-1, tile_size, feature_width)[row_ids]]
    convert_element_type x2 -> x0, local copies, waits for them, and re-layouts: 6.79 us -> none  [the longest x1 4.65 us: body(): forward_terms.astype(jnp.bfloat16)]
  transfers between devices with their start and end apart: 5 -> 0, of which waited for: 3 -> 0; matrix products, arithmetic and copies ran while one was open for 37% -> 0% of each run, Pallas kernels for 0% -> 0%
where the time goes in v1:
time: 108 us
  Pallas kernels  97.7 us (90%)
  local copies, waits for them, and re-layouts  5.5 us (5%)
  other arithmetic  3.3 us (3%)
  between operations  1.34 us (1%)
    pallas_call x1, Pallas kernels, body(): pl.pallas_call(functools.partial(kernel, slots, row_blocks, col_blocks, p...  97.7 us
    unnamed x3, local copies, waits for them, and re-layouts  4.81 us

profile of v1, /device:TPU:1, one launch (start us, length us, event | category | flops | bytes accessed | tf_op | source)
XLA Modules:
  0.0 107.8 jit_solution(5785219603109077418)
XLA Ops:
  1.3 0.7 select_add_fusion
  2.0 0.2 convert_reduce_fusion.1
  2.2 0.2 convert_reduce_fusion.3
  2.4 0.1 convert_reduce_fusion.6
  2.5 0.3 convert_reduce_fusion
  2.8 0.1 convert_reduce_fusion.4
  3.0 0.8 select_reduce_fusion.3
  3.8 0.8 select_reduce_fusion
  4.6 0.7 concatenate.3.tab
  5.3 97.7 %layer.1 = (bf16[1024,128]{1,0:T(8,128)(2,1)}, f32[128,128]{1,0:T(8,128)}, bf16[1024,128]{1,0:T(8,128)(2,1)}) custom-call(s32[1296]{0:T(1024)} %concatenate.3.tab, bf16[1024,128]{1,0:T(8,128)(2,1)} %bitcast.12, s32[1024,128]{1,0:T(8,128)} %bitcast.11, bf16[184,256,256]{2,1,0:T(8,128)(2,1)} %bitcast.10, bf16[128,128]{1,0:T(8,128)(2,1)} %w_hbm.1, ...), custom_call_target="tpu_custom_call" | custom-call | tf_op jit(solution)/shard_map/layer/pallas_call | solution.py:385
  103.0 1.7 %copy.15 = bf16[1,1024,128]{2,1,0:T(8,128)(2,1)} copy(bf16[1,1024,128]{2,1,0:T(8,128)(2,1)} %bitcast.15) | data formatting | bytes 524288
  104.7 1.5 %copy.16 = f32[128,128]{1,0:T(8,128)} copy(f32[128,128]{1,0:T(8,128)} %get-tuple-element.33) | data formatting | bytes 131072
  106.1 1.7 %copy.17 = bf16[1,1024,128]{2,1,0:T(8,128)(2,1)} copy(bf16[1,1024,128]{2,1,0:T(8,128)(2,1)} %bitcast.14) | data formatting | bytes 524288
  (4 shorter events, 0.0 us)

commit v2 on v1

v2 whole, which is shorter than its diff:
```python
import functools

import jax
import jax.numpy as jnp
from jax import lax
from jax.experimental import pallas as pl
from jax.experimental.pallas import tpu as pltpu
from jax.sharding import PartitionSpec as P

MESH = pl.DeviceIdType.MESH
F32 = jnp.float32
BF16 = jnp.bfloat16
UNROLL = 23
N_COPIES = 104
PAD = 256


def sorted_slots(rows, cols, count, row_blocks, col_blocks):
    n = rows.shape[1]
    across = lax.broadcasted_iota(jnp.int32, (n, n), 1)
    downward = lax.broadcasted_iota(jnp.int32, (n, n), 0)
    ids = across[0:1]
    down_ids = downward[:, 0:1]
    dead = ids >= count

    def column(row):
        return jnp.sum(jnp.where(across == downward, row, 0), axis=1, keepdims=True)

    def one(target, source, targets, sources):
        key = jnp.where(dead, targets * sources + ids, target * sources + source)
        goal = jnp.where(dead, targets, target)
        goal_c = column(goal)
        before = key < column(key)
        rank = jnp.sum(jnp.where(before, 1, 0), axis=1, keepdims=True)
        again = jnp.sum(jnp.where(before & (goal == goal_c), 1, 0), axis=1, keepdims=True)
        head = jnp.where(again == 0, 1, 0)
        packed = down_ids * 256 + column(source) * 2 + head
        order = jnp.sum(jnp.where(rank == across, packed, 0), axis=0, keepdims=True)
        upto = jnp.sum(jnp.where(goal_c <= across, 1, 0), axis=0, keepdims=True)
        some = jnp.sum(jnp.where(goal_c == across, 1, 0), axis=0, keepdims=True)
        return order, jnp.maximum(upto - 1, 0) * 2 + jnp.where(some > 0, 1, 0)

    order_f, last_f = one(rows, cols, row_blocks, col_blocks)
    order_b, last_b = one(cols, rows, col_blocks, row_blocks)
    return order_f, order_b, last_f, last_b


def kernel(
    slots, row_blocks, col_blocks, per, scale,
    feat_hbm, mask_hbm, w_hbm, cot_hbm, rows_hbm, cols_hbm, count_hbm, tiles_hbm,
    out_ref, wg_ref, ig_ref,
    feat_v, mask_v, w_v, cot_v, rows_v, cols_v, count_s, pair_v, tiles_v, tab_v, tab,
    hid, grd, prods, fpart, bpart, sib, xsum,
    ra, rb, fr, fl, zs, zb,
    acc_f, acc_b, agg, tb, ac, ax, ay, az, ws,
    send_sem, recv_sem, local_sem,
):
    r = lax.axis_index("row")
    c = lax.axis_index("col")
    zh, y = r // 4, lax.rem(r, 4)
    x, zl, core = c // 4, lax.rem(c // 2, 2), lax.rem(c, 2)

    def col_of(xx, zz, kk):
        return xx * 4 + zz * 2 + kk

    def at_x(step):
        return lax.rem(x + step, 4)

    def at_y(step):
        return lax.rem(y + step, 4)

    def x_dev(step):
        return {"row": r, "col": col_of(at_x(step), zl, core)}

    def y_dev(step):
        return {"row": zh * 4 + at_y(step), "col": c}

    sib_dev = {"row": r, "col": col_of(x, zl, 1 - core)}
    zl_dev = {"row": r, "col": col_of(x, 1 - zl, core)}
    zh_dev = {"row": (1 - zh) * 4 + y, "col": c}
    zz_dev = {"row": (1 - zh) * 4 + y, "col": col_of(x, 1 - zl, core)}
    right, left, up, down = x_dev(1), x_dev(3), y_dev(1), y_dev(3)
    peers = [sib_dev, right, left, x_dev(2), up, down, y_dev(2), zl_dev, zh_dev, zz_dev]

    barrier = pltpu.get_barrier_semaphore()
    for peer in peers:
        pl.semaphore_signal(barrier, inc=1, device_id=peer, device_id_type=MESH)

    loads = [
        (feat_hbm, feat_v), (mask_hbm, mask_v), (w_hbm, w_v), (cot_hbm, cot_v),
        (rows_hbm, rows_v), (cols_hbm, cols_v),
        (count_hbm, count_s), (tiles_hbm, tiles_v),
    ]
    loads = [pltpu.make_async_copy(src, dst, local_sem.at[i]) for i, (src, dst) in enumerate(loads)]
    for load in loads:
        load.start()

    made = []

    def send(src, dst, dev):
        i = len(made)
        copy = pltpu.make_async_remote_copy(
            src_ref=src, dst_ref=dst, send_sem=send_sem.at[i], recv_sem=recv_sem.at[i],
            device_id=dev, device_id_type=MESH,
        )
        copy.start()
        made.append(copy)
        return copy

    half = per // 2

    def col_shard(xx, zz, kk, first=0, size=per):
        return grd.at[pl.ds(col_of(xx, zz, kk) * per + first, size)]

    def row_shard(zz, yy, first=0, size=per):
        return hid.at[pl.ds((zz * 4 + yy) * per + first, size)]

    def share(ref, dev):
        return send(ref, ref, dev)

    first, second = (0, half), (half, half)

    loads[0].wait()
    loads[1].wait()
    for j in range(per):
        rows = slice(j * 256, (j + 1) * 256)
        hid[r * per + j] = feat_v[rows] * mask_v[rows].astype(F32).astype(BF16)

    pl.semaphore_wait(barrier, len(peers))

    def spread_y(zz):
        a = share(row_shard(zz, y, *first), up)
        b = share(row_shard(zz, y, *second), down)
        return a, b, [share(row_shard(zz, y, *second), up), share(row_shard(zz, y, *first), down)]

    def relay_y(a, b, zz):
        a.wait_recv()
        on = [share(row_shard(zz, at_y(3), *first), up)]
        b.wait_recv()
        on.append(share(row_shard(zz, at_y(1), *second), down))
        return on

    def spread_x(zz):
        a = share(col_shard(x, zz, core, *first), right)
        b = share(col_shard(x, zz, core, *second), left)
        rest = [share(col_shard(x, zz, core, *second), right), share(col_shard(x, zz, core, *first), left)]
        c_s.append(share(col_shard(x, zz, core), sib_dev))
        return a, b, rest

    def relay_x(a, b, zz):
        a.wait_recv()
        on = [share(col_shard(at_x(3), zz, core, *first), right)]
        b.wait_recv()
        on.append(share(col_shard(at_x(1), zz, core, *second), left))
        return on

    def cross_near(rest, zz):
        rest[0].wait_recv()
        c_s.append(share(col_shard(at_x(3), zz, core), sib_dev))
        rest[1].wait_recv()
        c_s.append(share(col_shard(at_x(1), zz, core), sib_dev))

    def cross_far(on, zz):
        for copy in on:
            copy.wait_recv()
        c_s.append(share(col_shard(at_x(2), zz, core), sib_dev))

    c_s = []
    ra_y, rb_y, r_rest = spread_y(zh)
    r_z = share(row_shard(zh, y), zh_dev)

    loads[2].wait()
    loads[3].wait()
    for j in range(per):
        block = lax.dot_general(
            w_v[...], cot_v[j * 256 : (j + 1) * 256], (((1,), (1,)), ((), ())), preferred_element_type=F32
        )
        grd[c * per + j] = block.astype(BF16)
    ca_x, cb_x, c_rest = spread_x(zl)

    for load in loads[4:7]:
        load.wait()
    pair_v[...] = jnp.zeros_like(pair_v)
    pair_v[0:1, 0:slots] = rows_v[...]
    pair_v[1:2, 0:slots] = cols_v[...]
    table = sorted_slots(pair_v[0:1], pair_v[1:2], count_s[0, 0], row_blocks, col_blocks)
    for i, line in enumerate(table):
        tab_v[i : i + 1] = line
    to_smem = pltpu.make_async_copy(tab_v, tab, local_sem.at[8])
    to_smem.start()

    r_on = relay_y(ra_y, rb_y, zh)
    c_on = relay_x(ca_x, cb_x, zl)
    r_z.wait_recv()
    za_y, zb_y, rz_rest = spread_y(1 - zh)
    c_z = share(col_shard(x, zl, core), zl_dev)
    cross_near(c_rest, zl)
    rz_on = relay_y(za_y, zb_y, 1 - zh)
    cross_far(c_on, zl)
    c_z.wait_recv()
    za_x, zb_x, cz_rest = spread_x(1 - zl)
    to_smem.wait()
    loads[7].wait()
    for copy in (*r_rest, *r_on, *rz_rest, *rz_on):
        copy.wait_recv()

    def fwd_range(lo, hi):
        @pl.loop(lo, hi)
        def _(g):
            acc = acc_f[...]
            for u in range(UNROLL):
                p = g * UNROLL + u
                word = tab[0, p]
                prod = jnp.dot(tiles_v[word >> 8], hid[(word >> 1) & 127], preferred_element_type=F32)
                acc = jnp.where((word & 1) == 1, 0.0, acc) + prod
                prods[p] = acc.astype(BF16)
            acc_f[...] = acc

    def bwd_range(lo, hi):
        @pl.loop(lo, hi)
        def _(g):
            acc = acc_b[...]
            for u in range(UNROLL):
                p = g * UNROLL + u
                word = tab[1, p]
                prod = jnp.dot(grd[(word >> 1) & 127], tiles_v[word >> 8], preferred_element_type=F32)
                acc = jnp.where((word & 1) == 1, 0.0, acc) + prod
                prods[p, 0:128, :] = acc[:, 0:128].astype(BF16)
                prods[p, 128:256, :] = acc[:, 128:256].astype(BF16)
            acc_b[...] = acc

    groups = slots // UNROLL
    acc_f[...] = jnp.zeros_like(acc_f)
    acc_b[...] = jnp.zeros_like(acc_b)

    fwd_range(0, groups // 4)
    cz_on = relay_x(za_x, zb_x, 1 - zl)
    cross_near(cz_rest, 1 - zl)
    fwd_range(groups // 4, groups)
    cross_far(cz_on, 1 - zl)

    def take(dst, line, base):
        for j in range(per):
            word = tab[line, base + j]
            value = prods[word >> 1]
            dst[base + j] = jnp.where((word & 1) == 1, value, jnp.zeros_like(value))

    zs_of = (1 - zl, zl)
    sibs = {}
    for dz in range(2):
        for dx in (2, 1, 3, 0):
            base = col_of(at_x(dx), zs_of[dz], 1 - core) * per
            take(fpart, 2, base)
            sibs[dz, dx] = send(fpart.at[pl.ds(base, per)], sib.at[dz, dx], sib_dev)

    @pl.loop(0, row_blocks // (2 * per))
    def _(m):
        take(fpart, 2, (2 * m + core) * per)

    def with_sibling(dz, dx):
        sibs[dz, dx].wait_recv()
        base = col_of(at_x(dx), zs_of[dz], core) * per
        for j in range(per):
            xsum[dz, dx, j] = (fpart[base + j].astype(F32) + sib[dz, dx, j].astype(F32)).astype(BF16)

    def add_into(dst, start, other):
        for j in range(half):
            dst[start + j] = (dst[start + j].astype(F32) + other[j].astype(F32)).astype(BF16)

    def ring_sum(k, part, prepare, ahead, behind, z_dev, finish):
        a, b = first, second

        def piece(dz, d, ab):
            return part(dz, d).at[pl.ds(ab[0], ab[1])]

        outer, inner = {}, {}

        def far(dz):
            prepare(dz, 2)
            outer[dz] = (
                send(piece(dz, 2, a), ra.at[k, dz], ahead),
                send(piece(dz, 2, b), rb.at[k, dz], behind),
            )

        def near(dz):
            prepare(dz, 1)
            prepare(dz, 3)
            inner[dz] = [
                send(piece(dz, 1, b), fr.at[k, dz, pl.ds(half, half)], ahead),
                send(piece(dz, 3, a), fl.at[k, dz, pl.ds(0, half)], behind),
            ]

        def relay(dz):
            outer[dz][0].wait_recv()
            add_into(part(dz, 1), 0, ra.at[k, dz])
            inner[dz].append(send(piece(dz, 1, a), fr.at[k, dz, pl.ds(0, half)], ahead))
            outer[dz][1].wait_recv()
            add_into(part(dz, 3), half, rb.at[k, dz])
            inner[dz].append(send(piece(dz, 3, b), fl.at[k, dz, pl.ds(half, half)], behind))

        def total(dz, j):
            return part(dz, 0)[j].astype(F32) + fr[k, dz, j].astype(F32) + fl[k, dz, j].astype(F32)

        far(0)
        near(0)
        yield
        relay(0)
        far(1)
        near(1)
        prepare(0, 0)
        yield
        for copy in inner[0]:
            copy.wait_recv()
        for j in range(per):
            zs[k, j] = total(0, j).astype(BF16)
        last = send(zs.at[k], zb.at[k], z_dev)
        prepare(1, 0)
        yield
        relay(1)
        yield
        for copy in inner[1]:
            copy.wait_recv()
        last.wait_recv()
        for j in range(per):
            finish(j, total(1, j) + zb[k, j].astype(F32))

    def finish_f(j, value):
        agg[j * 256 : (j + 1) * 256] = value.astype(BF16)

    def finish_b(j, value):
        for h in range(2):
            rows = slice(j * 256 + h * 128, j * 256 + h * 128 + 128)
            ig_ref[rows] = (value[h * 128 : (h + 1) * 128].T * mask_v[rows].astype(F32)).astype(BF16)

    sum_f = ring_sum(0, lambda dz, d: xsum.at[dz, d], with_sibling, right, left, zl_dev, finish_f)

    zh_of = (1 - zh, zh)
    sum_b = ring_sum(
        1,
        lambda dz, d: bpart.at[pl.ds((zh_of[dz] * 4 + at_y(d)) * per, per)],
        lambda dz, d: None,
        up, down, zh_dev, finish_b,
    )

    for copy in c_s:
        copy.wait_recv()
    bwd_range(0, groups // 4)
    next(sum_f)
    bwd_range(groups // 4, groups)

    @pl.loop(0, col_blocks // per)
    def _(m):
        take(bpart, 3, m * per)

    next(sum_b)
    next(sum_f)
    next(sum_b)
    next(sum_f)
    next(sum_f)
    next(sum_b)
    next(sum_b)
    next(sum_f, None)

    tb[...] = lax.dot_general(agg[...], cot_v[...], (((0,), (0,)), ((), ())), preferred_element_type=F32)
    rows = tb.shape[0] // 2
    to_sib = send(tb.at[pl.ds((1 - core) * rows, rows)], ac, sib_dev)
    out_ref[...] = jnp.dot(agg[...], w_v[...], preferred_element_type=F32).astype(BF16)
    to_sib.wait_recv()

    def ring_add(slots_ref, at, value, devices):
        slots_ref[at] = value
        copies = [send(slots_ref.at[at], slots_ref.at[at], dev) for dev in devices]
        for copy in copies:
            copy.wait_recv()
        return (slots_ref[0] + slots_ref[1]) + (slots_ref[2] + slots_ref[3])

    term = tb[pl.ds(core * rows, rows)] + ac[...]
    term = ring_add(ax, x, term, [x_dev(step) for step in (1, 3, 2)])
    term = ring_add(az, zh * 2 + zl, term, [zl_dev, zh_dev, zz_dev])
    term = ring_add(ay, y, term, [y_dev(step) for step in (1, 3, 2)])
    ws[core] = term * scale
    last = share(ws.at[core], sib_dev)
    next(sum_b, None)
    last.wait_recv()
    wg_ref[0:rows] = ws[0]
    wg_ref[rows : 2 * rows] = ws[1]

    for copy in made:
        copy.wait_send()


def body(features, relu_mask, tiles, tile_rows, tile_cols, tile_count, weight, cotangent):
    slots, tile = tiles.shape[2], tiles.shape[3]
    own, width = features.shape[1:]
    per = own // tile
    row_blocks, col_blocks = per * lax.axis_size("col"), per * lax.axis_size("row")
    half = per // 2
    scale = float((own * lax.axis_size("row") * lax.axis_size("col")) ** -0.5)
    block = (tile, width)
    v = pltpu.VMEM
    anywhere = pl.BlockSpec(memory_space=pl.ANY)
    in_vmem = pl.BlockSpec(memory_space=pltpu.VMEM)
    out_pre, weight_grad, input_grad = pl.pallas_call(
        functools.partial(kernel, slots, row_blocks, col_blocks, per, scale),
        out_shape=(
            jax.ShapeDtypeStruct((own, width), BF16),
            jax.ShapeDtypeStruct((width, width), F32),
            jax.ShapeDtypeStruct((own, width), BF16),
        ),
        in_specs=[anywhere] * 8,
        out_specs=(in_vmem,) * 3,
        scratch_shapes=[
            v((own, width), BF16),
            v((own, width), jnp.int32),
            v((width, width), BF16),
            v((own, width), BF16),
            v((1, slots), jnp.int32),
            v((1, slots), jnp.int32),
            pltpu.SMEM((1, 1), jnp.int32),
            v((8, PAD), jnp.int32),
            v((slots, tile, tile), BF16),
            v((8, PAD), jnp.int32),
            pltpu.SMEM((8, PAD), jnp.int32),
            v((col_blocks,) + block, BF16),
            v((row_blocks, width, tile), BF16),
            v((slots,) + block, BF16),
            v((row_blocks,) + block, BF16),
            v((col_blocks,) + block, BF16),
            v((2, 4, per) + block, BF16),
            v((2, 4, per) + block, BF16),
            v((2, 2, half) + block, BF16),
            v((2, 2, half) + block, BF16),
            v((2, 2, per) + block, BF16),
            v((2, 2, per) + block, BF16),
            v((2, per) + block, BF16),
            v((2, per) + block, BF16),
            v(block, F32),
            v((width, tile), F32),
            v((own, width), BF16),
            v((width, width), F32),
            v((width // 2, width), F32),
            v((4, width // 2, width), F32),
            v((4, width // 2, width), F32),
            v((4, width // 2, width), F32),
            v((2, width // 2, width), F32),
            pltpu.SemaphoreType.DMA((N_COPIES,)),
            pltpu.SemaphoreType.DMA((N_COPIES,)),
            pltpu.SemaphoreType.DMA((9,)),
        ],
        compiler_params=pltpu.CompilerParams(
            collective_id=0, has_side_effects=True, vmem_limit_bytes=67043328
        ),
        name="layer",
    )(features[0], relu_mask[0], weight, cotangent[0], tile_rows[0], tile_cols[0], tile_count, tiles[0, 0])
    return out_pre[None], weight_grad, input_grad[None]


def solution(mesh):
    placed = (
        P("col", "row", None),
        P("col", "row", None),
        P("row", "col", None, None, None),
        P("row", "col", None),
        P("row", "col", None),
        P("row", "col"),
        P(),
        P("row", "col", None),
    )
    return jax.shard_map(
        body,
        mesh=mesh,
        in_specs=placed,
        out_specs=(P("row", "col", None), P(), P("col", "row", None)),
        check_vma=False,
    )
```

time: 108 us -> 80.8 us (0.75)
  Pallas kernels: 97.7 us -> 74.5 us
  other arithmetic: 3.3 us -> 0 us
    pallas_call x1, Pallas kernels: 97.7 us -> 74.5 us  [body(): pl.pallas_call(functools.partial(kernel, slots, row_blocks, col_blocks, p...]
    reduce_sum x6 -> x0, other arithmetic: 2.28 us -> none  [the longest x2 1.67 us: permute(): return jnp.sum(jnp.where(hit, values[:, None], 0), axis=0)]
where the time goes in v2:
time: 80.8 us; the launch traced here: 80.6 us
  Pallas kernels  74.5 us (92%)
  local copies, waits for them, and re-layouts  4.81 us (6%)
  between operations  1.29 us (2%)
    pallas_call x1, Pallas kernels, body(): pl.pallas_call(functools.partial(kernel, slots, row_blocks, col_blocks, p...  74.5 us
    unnamed x3, local copies, waits for them, and re-layouts  4.81 us

profile of v2, /device:TPU:1, one launch (start us, length us, event | category | flops | bytes accessed | tf_op | source)
XLA Modules:
  0.0 80.6 jit_solution(13682907682513641919)
XLA Ops:
  1.3 74.5 %layer.1 = (bf16[1024,128]{1,0:T(8,128)(2,1)}, f32[128,128]{1,0:T(8,128)}, bf16[1024,128]{1,0:T(8,128)(2,1)}) custom-call(bf16[1024,128]{1,0:T(8,128)(2,1)} %bitcast.10, s32[1024,128]{1,0:T(8,128)} %bitcast.9, bf16[128,128]{1,0:T(8,128)(2,1)} %w_hbm.1, bf16[1024,128]{1,0:T(8,128)(2,1)} %bitcast.11, s32[1,184]{1,0:T(1,128)} %bitcast.14, s32[1,184]{1,0:T(1,128)} %bitcast.15, ...), custom_call_target="tpu_custom_call" | custom-call | tf_op jit(solution)/shard_map/layer/pallas_call | solution.py:403
  75.7 1.7 %copy.15 = bf16[1,1024,128]{2,1,0:T(8,128)(2,1)} copy(bf16[1,1024,128]{2,1,0:T(8,128)(2,1)} %bitcast.13) | data formatting | bytes 524288
  77.4 1.5 %copy.16 = f32[128,128]{1,0:T(8,128)} copy(f32[128,128]{1,0:T(8,128)} %get-tuple-element.13) | data formatting | bytes 131072
  78.9 1.7 %copy.17 = bf16[1,1024,128]{2,1,0:T(8,128)(2,1)} copy(bf16[1,1024,128]{2,1,0:T(8,128)(2,1)} %bitcast.12) | data formatting | bytes 524288

commit v3 on v2

--- a/solution.py
+++ b/solution.py
@@ -10,8 +10,8 @@
 MESH = pl.DeviceIdType.MESH
 F32 = jnp.float32
 BF16 = jnp.bfloat16
-UNROLL = 23
-N_COPIES = 104
+UNROLL = 46
+N_COPIES = 128
 PAD = 256
 
 
@@ -51,8 +51,8 @@
     out_ref, wg_ref, ig_ref,
     feat_v, mask_v, w_v, cot_v, rows_v, cols_v, count_s, pair_v, tiles_v, tab_v, tab,
     hid, grd, prods, fpart, bpart, sib, xsum,
-    ra, rb, fr, fl, zs, zb,
-    acc_f, acc_b, agg, tb, ac, ax, ay, az, ws,
+    f_ra, f_rb, f_fr, f_fl, f_zs, f_zb, b_ra, b_rb, b_fr, b_fl, b_zs, b_zb,
+    acc_f, acc_b, tb, ac, ax, ay, az, ws,
     send_sem, recv_sem, local_sem,
 ):
     r = lax.axis_index("row")
@@ -92,7 +92,7 @@
         (count_hbm, count_s), (tiles_hbm, tiles_v),
     ]
     loads = [pltpu.make_async_copy(src, dst, local_sem.at[i]) for i, (src, dst) in enumerate(loads)]
-    for load in loads:
+    for load in loads[:7]:
         load.start()
 
     made = []
@@ -122,6 +122,7 @@
 
     loads[0].wait()
     loads[1].wait()
+    loads[7].start()
     for j in range(per):
         rows = slice(j * 256, (j + 1) * 256)
         hid[r * per + j] = feat_v[rows] * mask_v[rows].astype(F32).astype(BF16)
@@ -165,18 +166,37 @@
             copy.wait_recv()
         c_s.append(share(col_shard(at_x(2), zz, core), sib_dev))
 
+    def half_y(zz, ab):
+        return share(row_shard(zz, y, *ab), up), share(row_shard(zz, y, *ab), down)
+
+    def half_x(zz, ab):
+        return share(col_shard(x, zz, core, *ab), right), share(col_shard(x, zz, core, *ab), left)
+
+    def pass_y(copy, zz, ab, step, dev):
+        copy.wait_recv()
+        return share(row_shard(zz, at_y(step), *ab), dev)
+
+    def pass_x(copy, zz, ab, step, dev):
+        copy.wait_recv()
+        return share(col_shard(at_x(step), zz, core, *ab), dev)
+
     c_s = []
     ra_y, rb_y, r_rest = spread_y(zh)
-    r_z = share(row_shard(zh, y), zh_dev)
+    r_za = share(row_shard(zh, y, *first), zh_dev)
 
     loads[2].wait()
     loads[3].wait()
+    unit = lax.broadcasted_iota(jnp.int32, w_v.shape, 0) == lax.broadcasted_iota(jnp.int32, w_v.shape, 1)
+    unit = jnp.where(unit, 1.0, 0.0).astype(BF16)
     for j in range(per):
         block = lax.dot_general(
-            w_v[...], cot_v[j * 256 : (j + 1) * 256], (((1,), (1,)), ((), ())), preferred_element_type=F32
+            unit, cot_v[j * 256 : (j + 1) * 256], (((1,), (1,)), ((), ())), preferred_element_type=F32
         )
         grd[c * per + j] = block.astype(BF16)
     ca_x, cb_x, c_rest = spread_x(zl)
+    c_za = share(col_shard(x, zl, core, *first), zl_dev)
+    r_zb = share(row_shard(zh, y, *second), zh_dev)
+    c_zb = share(col_shard(x, zl, core, *second), zl_dev)
 
     for load in loads[4:7]:
         load.wait()
@@ -191,29 +211,40 @@
 
     r_on = relay_y(ra_y, rb_y, zh)
     c_on = relay_x(ca_x, cb_x, zl)
-    r_z.wait_recv()
-    za_y, zb_y, rz_rest = spread_y(1 - zh)
-    c_z = share(col_shard(x, zl, core), zl_dev)
+    r_za.wait_recv()
+    rza_u, rza_d = half_y(1 - zh, first)
+    c_za.wait_recv()
+    cza_r, cza_l = half_x(1 - zl, first)
     cross_near(c_rest, zl)
-    rz_on = relay_y(za_y, zb_y, 1 - zh)
+    r_zb.wait_recv()
+    rzb_u, rzb_d = half_y(1 - zh, second)
     cross_far(c_on, zl)
-    c_z.wait_recv()
-    za_x, zb_x, cz_rest = spread_x(1 - zl)
+    c_zb.wait_recv()
+    czb_r, czb_l = half_x(1 - zl, second)
+    c_s.append(share(col_shard(x, 1 - zl, core), sib_dev))
+    rz_on = [pass_y(rza_u, 1 - zh, first, 3, up)]
+    cz_on = [pass_x(cza_r, 1 - zl, first, 3, right)]
+    rz_on.append(pass_y(rzb_d, 1 - zh, second, 1, down))
+    cz_on.append(pass_x(czb_l, 1 - zl, second, 1, left))
+    cz_rest = (czb_r, cza_l)
     to_smem.wait()
     loads[7].wait()
-    for copy in (*r_rest, *r_on, *rz_rest, *rz_on):
+    for copy in (*r_rest, *r_on, rzb_u, rza_d, *rz_on):
         copy.wait_recv()
 
-    def fwd_range(lo, hi):
+    low, high = slice(0, 128), slice(128, 256)
+    parts = (low, high)
+
+    def fwd_range(h, lo, hi):
         @pl.loop(lo, hi)
         def _(g):
             acc = acc_f[...]
             for u in range(UNROLL):
                 p = g * UNROLL + u
                 word = tab[0, p]
-                prod = jnp.dot(tiles_v[word >> 8], hid[(word >> 1) & 127], preferred_element_type=F32)
+                prod = jnp.dot(tiles_v[word >> 8, parts[h], :], hid[(word >> 1) & 127], preferred_element_type=F32)
                 acc = jnp.where((word & 1) == 1, 0.0, acc) + prod
-                prods[p] = acc.astype(BF16)
+                prods[p, parts[h], :] = acc.astype(BF16)
             acc_f[...] = acc
 
     def bwd_range(lo, hi):
@@ -225,49 +256,45 @@
                 word = tab[1, p]
                 prod = jnp.dot(grd[(word >> 1) & 127], tiles_v[word >> 8], preferred_element_type=F32)
                 acc = jnp.where((word & 1) == 1, 0.0, acc) + prod
-                prods[p, 0:128, :] = acc[:, 0:128].astype(BF16)
-                prods[p, 128:256, :] = acc[:, 128:256].astype(BF16)
+                prods[p, low, :] = acc[:, low].astype(BF16)
+                prods[p, high, :] = acc[:, high].astype(BF16)
             acc_b[...] = acc
 
     groups = slots // UNROLL
     acc_f[...] = jnp.zeros_like(acc_f)
     acc_b[...] = jnp.zeros_like(acc_b)
 
-    fwd_range(0, groups // 4)
-    cz_on = relay_x(za_x, zb_x, 1 - zl)
-    cross_near(cz_rest, 1 - zl)
-    fwd_range(groups // 4, groups)
-    cross_far(cz_on, 1 - zl)
-
-    def take(dst, line, base):
-        for j in range(per):
-            word = tab[line, base + j]
-            value = prods[word >> 1]
-            dst[base + j] = jnp.where((word & 1) == 1, value, jnp.zeros_like(value))
-
     zs_of = (1 - zl, zl)
     sibs = {}
-    for dz in range(2):
-        for dx in (2, 1, 3, 0):
-            base = col_of(at_x(dx), zs_of[dz], 1 - core) * per
-            take(fpart, 2, base)
-            sibs[dz, dx] = send(fpart.at[pl.ds(base, per)], sib.at[dz, dx], sib_dev)
-
-    @pl.loop(0, row_blocks // (2 * per))
-    def _(m):
-        take(fpart, 2, (2 * m + core) * per)
-
-    def with_sibling(dz, dx):
-        sibs[dz, dx].wait_recv()
+
+    def take_f(h, base):
+        for j in range(per):
+            word = tab[2, base + j]
+            value = prods[word >> 1, parts[h], :]
+            fpart[h, base + j] = jnp.where((word & 1) == 1, value, jnp.zeros_like(value))
+
+    def fill_f(h):
+        for dz in range(2):
+            for dx in (2, 1, 3, 0):
+                base = col_of(at_x(dx), zs_of[dz], 1 - core) * per
+                take_f(h, base)
+                sibs[h, dz, dx] = send(fpart.at[h, pl.ds(base, per)], sib.at[h, dz, dx], sib_dev)
+
+        @pl.loop(0, row_blocks // (2 * per))
+        def _(m):
+            take_f(h, (2 * m + core) * per)
+
+    def with_sibling(h, dz, dx):
+        sibs[h, dz, dx].wait_recv()
         base = col_of(at_x(dx), zs_of[dz], core) * per
         for j in range(per):
-            xsum[dz, dx, j] = (fpart[base + j].astype(F32) + sib[dz, dx, j].astype(F32)).astype(BF16)
+            xsum[h, dz, dx, j] = (fpart[h, base + j].astype(F32) + sib[h, dz, dx, j].astype(F32)).astype(BF16)
 
     def add_into(dst, start, other):
         for j in range(half):
             dst[start + j] = (dst[start + j].astype(F32) + other[j].astype(F32)).astype(BF16)
 
-    def ring_sum(k, part, prepare, ahead, behind, z_dev, finish):
+    def ring_sum(ra, rb, fr, fl, zs, zb, part, prepare, ahead, behind, z_dev, finish):
         a, b = first, second
 
         def piece(dz, d, ab):
@@ -275,45 +302,42 @@
 
         outer, inner = {}, {}
 
-        def far(dz):
+        def spread(dz):
             prepare(dz, 2)
             outer[dz] = (
-                send(piece(dz, 2, a), ra.at[k, dz], ahead),
-                send(piece(dz, 2, b), rb.at[k, dz], behind),
+                send(piece(dz, 2, a), ra.at[dz], ahead),
+                send(piece(dz, 2, b), rb.at[dz], behind),
             )
-
-        def near(dz):
             prepare(dz, 1)
             prepare(dz, 3)
             inner[dz] = [
-                send(piece(dz, 1, b), fr.at[k, dz, pl.ds(half, half)], ahead),
-                send(piece(dz, 3, a), fl.at[k, dz, pl.ds(0, half)], behind),
+                send(piece(dz, 1, b), fr.at[dz, pl.ds(half, half)], ahead),
+                send(piece(dz, 3, a), fl.at[dz, pl.ds(0, half)], behind),
             ]
 
         def relay(dz):
             outer[dz][0].wait_recv()
-            add_into(part(dz, 1), 0, ra.at[k, dz])
-            inner[dz].append(send(piece(dz, 1, a), fr.at[k, dz, pl.ds(0, half)], ahead))
+            add_into(part(dz, 1), 0, ra.at[dz])
+            inner[dz].append(send(piece(dz, 1, a), fr.at[dz, pl.ds(0, half)], ahead))
             outer[dz][1].wait_recv()
-            add_into(part(dz, 3), half, rb.at[k, dz])
-            inner[dz].append(send(piece(dz, 3, b), fl.at[k, dz, pl.ds(half, half)], behind))
+            add_into(part(dz, 3), half, rb.at[dz])
+            inner[dz].append(send(piece(dz, 3, b), fl.at[dz, pl.ds(half, half)], behind))
 
         def total(dz, j):
-            return part(dz, 0)[j].astype(F32) + fr[k, dz, j].astype(F32) + fl[k, dz, j].astype(F32)
-
-        far(0)
-        near(0)
+            return part(dz, 0)[j].astype(F32) + fr[dz, j].astype(F32) + fl[dz, j].astype(F32)
+
+        spread(0)
         yield
         relay(0)
-        far(1)
-        near(1)
+        yield
+        spread(1)
         prepare(0, 0)
         yield
         for copy in inner[0]:
             copy.wait_recv()
         for j in range(per):
-            zs[k, j] = total(0, j).astype(BF16)
-        last = send(zs.at[k], zb.at[k], z_dev)
+            zs[j] = total(0, j).astype(BF16)
+        last = send(zs, zb, z_dev)
         prepare(1, 0)
         yield
         relay(1)
@@ -322,71 +346,131 @@
             copy.wait_recv()
         last.wait_recv()
         for j in range(per):
-            finish(j, total(1, j) + zb[k, j].astype(F32))
-
-    def finish_f(j, value):
-        agg[j * 256 : (j + 1) * 256] = value.astype(BF16)
+            finish(j, total(1, j) + zb[j].astype(F32))
+
+    def forward_sum(h):
+        def finish(j, value):
+            rows = slice(j * 256 + h * 128, j * 256 + h * 128 + 128)
+            out_ref[rows] = jnp.dot(value.astype(BF16), w_v[...], preferred_element_type=F32).astype(BF16)
+
+        return ring_sum(
+            f_ra.at[h], f_rb.at[h], f_fr.at[h], f_fl.at[h], f_zs.at[h], f_zb.at[h],
+            lambda dz, d: xsum.at[h, dz, d],
+            functools.partial(with_sibling, h),
+            right, left, zl_dev, finish,
+        )
 
     def finish_b(j, value):
         for h in range(2):
             rows = slice(j * 256 + h * 128, j * 256 + h * 128 + 128)
-            ig_ref[rows] = (value[h * 128 : (h + 1) * 128].T * mask_v[rows].astype(F32)).astype(BF16)
-
-    sum_f = ring_sum(0, lambda dz, d: xsum.at[dz, d], with_sibling, right, left, zl_dev, finish_f)
+            grad = lax.dot_general(
+                value[parts[h]].astype(BF16), w_v[...], (((0,), (1,)), ((), ())), preferred_element_type=F32
+            )
+            ig_ref[rows] = (grad * mask_v[rows].astype(F32)).astype(BF16)
 
     zh_of = (1 - zh, zh)
     sum_b = ring_sum(
-        1,
+        b_ra, b_rb, b_fr, b_fl, b_zs, b_zb,
         lambda dz, d: bpart.at[pl.ds((zh_of[dz] * 4 + at_y(d)) * per, per)],
         lambda dz, d: None,
         up, down, zh_dev, finish_b,
     )
 
+    def weight_sum():
+        tb[...] = jnp.zeros_like(tb)
+
+        @pl.loop(0, col_blocks // 16)
+        def _(g):
+            acc = tb[...]
+            for u in range(16):
+                i = g * 16 + u
+                columns = jnp.concatenate([bpart[i, low, :], bpart[i, high, :]], axis=1)
+                acc += jnp.dot(columns, hid[i], preferred_element_type=F32)
+            tb[...] = acc
+
+        rows = tb.shape[0] // 2
+        to_sib = send(tb.at[pl.ds((1 - core) * rows, rows)], ac, sib_dev)
+        yield
+        to_sib.wait_recv()
+        term = tb[pl.ds(core * rows, rows)] + ac[...]
+        stages = (
+            (az, zh * 2 + zl, [zl_dev, zh_dev, zz_dev]),
+            (ax, x, [x_dev(step) for step in (1, 3, 2)]),
+            (ay, y, [y_dev(step) for step in (1, 3, 2)]),
+        )
+        for held, at, devices in stages:
+            held[at] = term
+            copies = [send(held.at[at], held.at[at], dev) for dev in devices]
+            yield
+            for copy in copies:
+                copy.wait_recv()
+            term = (held[0] + held[1]) + (held[2] + held[3])
+        ws[core] = term * scale
+        last = share(ws.at[core], sib_dev)
+        yield
+        last.wait_recv()
+        wg_ref[...] = jnp.concatenate([ws[0], ws[1]], axis=0).T
+
+    f_lo, f_hi, wsum = forward_sum(0), forward_sum(1), weight_sum()
+
+    fwd_range(0, 0, groups // 2)
+    cross_near(cz_rest, 1 - zl)
+    fwd_range(0, groups // 2, groups)
+    fill_f(0)
+    cross_far(cz_on, 1 - zl)
     for copy in c_s:
         copy.wait_recv()
-    bwd_range(0, groups // 4)
-    next(sum_f)
-    bwd_range(groups // 4, groups)
+
+    bwd_range(0, groups // 2)
+    next(f_lo)
+    bwd_range(groups // 2, groups)
 
     @pl.loop(0, col_blocks // per)
     def _(m):
-        take(bpart, 3, m * per)
+        for j in range(per):
+            word = tab[3, m * per + j]
+            value = prods[word >> 1]
+            bpart[m * per + j] = jnp.where((word & 1) == 1, value, jnp.zeros_like(value))
 
     next(sum_b)
-    next(sum_f)
+    next(wsum)
+    fwd_range(1, 0, groups // 4)
+    next(f_lo)
+    next(wsum)
+    next(f_lo)
+    fwd_range(1, groups // 4, groups // 2)
+    next(wsum)
+    fwd_range(1, groups // 2, groups)
     next(sum_b)
-    next(sum_f)
-    next(sum_f)
+    fill_f(1)
+    next(f_lo)
+    next(f_lo)
+    next(f_hi)
     next(sum_b)
+    next(wsum)
+    next(f_hi)
+    next(f_hi)
     next(sum_b)
-    next(sum_f, None)
-
-    tb[...] = lax.dot_general(agg[...], cot_v[...], (((0,), (0,)), ((), ())), preferred_element_type=F32)
-    rows = tb.shape[0] // 2
-    to_sib = send(tb.at[pl.ds((1 - core) * rows, rows)], ac, sib_dev)
-    out_ref[...] = jnp.dot(agg[...], w_v[...], preferred_element_type=F32).astype(BF16)
-    to_sib.wait_recv()
-
-    def ring_add(slots_ref, at, value, devices):
-        slots_ref[at] = value
-        copies = [send(slots_ref.at[at], slots_ref.at[at], dev) for dev in devices]
-        for copy in copies:
-            copy.wait_recv()
-        return (slots_ref[0] + slots_ref[1]) + (slots_ref[2] + slots_ref[3])
-
-    term = tb[pl.ds(core * rows, rows)] + ac[...]
-    term = ring_add(ax, x, term, [x_dev(step) for step in (1, 3, 2)])
-    term = ring_add(az, zh * 2 + zl, term, [zl_dev, zh_dev, zz_dev])
-    term = ring_add(ay, y, term, [y_dev(step) for step in (1, 3, 2)])
-    ws[core] = term * scale
-    last = share(ws.at[core], sib_dev)
+    next(f_lo, None)
+    next(f_hi)
+    next(sum_b)
+    next(f_hi)
+    next(wsum)
+    next(f_hi, None)
+    next(wsum, None)
     next(sum_b, None)
-    last.wait_recv()
-    wg_ref[0:rows] = ws[0]
-    wg_ref[rows : 2 * rows] = ws[1]
 
     for copy in made:
         copy.wait_send()
+
+
+def keep(a_ref, b_ref, c_ref, a_out, b_out, c_out, sem):
+    pairs = ((a_ref, a_out), (b_ref, b_out), (c_ref, c_out))
+    copies = [pltpu.make_async_copy(src, dst, sem.at[i]) for i, (src, dst) in enumerate(pairs)]
+    for copy in copies:
+        copy.start()
+    for copy in copies:
+        copy.wait()
 
 
 def body(features, relu_mask, tiles, tile_rows, tile_cols, tile_count, weight, cotangent):
@@ -396,11 +480,16 @@
     row_blocks, col_blocks = per * lax.axis_size("col"), per * lax.axis_size("row")
     half = per // 2
     scale = float((own * lax.axis_size("row") * lax.axis_size("col")) ** -0.5)
-    block = (tile, width)
+    block, small = (tile, width), (tile // 2, width)
     v = pltpu.VMEM
+
+    def ring_buffers(lead, rows):
+        shapes = [(2, half), (2, half), (2, per), (2, per), (per,), (per,)]
+        return [v(lead + shape + rows, BF16) for shape in shapes]
+
     anywhere = pl.BlockSpec(memory_space=pl.ANY)
     in_vmem = pl.BlockSpec(memory_space=pltpu.VMEM)
-    out_pre, weight_grad, input_grad = pl.pallas_call(
+    results = pl.pallas_call(
         functools.partial(kernel, slots, row_blocks, col_blocks, per, scale),
         out_shape=(
             jax.ShapeDtypeStruct((own, width), BF16),
@@ -424,19 +513,14 @@
             v((col_blocks,) + block, BF16),
             v((row_blocks, width, tile), BF16),
             v((slots,) + block, BF16),
-            v((row_blocks,) + block, BF16),
+            v((2, row_blocks) + small, BF16),
             v((col_blocks,) + block, BF16),
-            v((2, 4, per) + block, BF16),
-            v((2, 4, per) + block, BF16),
-            v((2, 2, half) + block, BF16),
-            v((2, 2, half) + block, BF16),
-            v((2, 2, per) + block, BF16),
-            v((2, 2, per) + block, BF16),
-            v((2, per) + block, BF16),
-            v((2, per) + block, BF16),
-            v(block, F32),
+            v((2, 2, 4, per) + small, BF16),
+            v((2, 2, 4, per) + small, BF16),
+            *ring_buffers((2,), small),
+            *ring_buffers((), block),
+            v(small, F32),
             v((width, tile), F32),
-            v((own, width), BF16),
             v((width, width), F32),
             v((width // 2, width), F32),
             v((4, width // 2, width), F32),
@@ -452,6 +536,15 @@
         ),
         name="layer",
     )(features[0], relu_mask[0], weight, cotangent[0], tile_rows[0], tile_cols[0], tile_count, tiles[0, 0])
+    out_pre, weight_grad, input_grad = pl.pallas_call(
+        keep,
+        out_shape=[jax.ShapeDtypeStruct(value.shape, value.dtype) for value in results],
+        in_specs=[in_vmem] * 3,
+        out_specs=[anywhere] * 3,
+        scratch_shapes=[pltpu.SemaphoreType.DMA((3,))],
+        compiler_params=pltpu.CompilerParams(vmem_limit_bytes=4 * 1024 * 1024),
+        name="keep",
+    )(*results)
     return out_pre[None], weight_grad, input_grad[None]
 
 

time: 80.8 us -> 71.3 us (0.88)
  Pallas kernels: 74.5 us -> 66.3 us
  local copies, waits for them, and re-layouts: 4.81 us -> 2.73 us
    pallas_call x1, Pallas kernels: 74.5 us -> 65.4 us  [body(): pl.pallas_call(functools.partial(kernel, slots, row_blocks, col_blocks, p...]
    unnamed x3 -> x6, local copies, waits for them, and re-layouts: 4.81 us -> 2.73 us
    pallas_call x0 -> x1, Pallas kernels: none -> 0.83 us  [body(): pl.pallas_call(keep, out_shape=[jax.ShapeDtypeStruct(value.shape, value.d...]
where the time goes in v3:
time: 71.3 us; the launch traced here: 70.3 us
  Pallas kernels  66.3 us (93%)
  local copies, waits for them, and re-layouts  2.73 us (4%)
  between operations  1.3 us (2%)
    pallas_call x1, Pallas kernels, body(): pl.pallas_call(functools.partial(kernel, slots, row_blocks, col_blocks, p...  65.4 us
    unnamed x6, local copies, waits for them, and re-layouts  2.73 us

profile of v3, /device:TPU:1, one launch (start us, length us, event | category | flops | bytes accessed | tf_op | source)
XLA Modules:
  0.0 70.3 jit_solution(2082957623206130630)
XLA Ops:
  1.3 65.4 %layer.1 = (bf16[1024,128]{1,0:T(8,128)(2,1)}, f32[128,128]{1,0:T(8,128)}, bf16[1024,128]{1,0:T(8,128)(2,1)}) custom-call(bf16[1024,128]{1,0:T(8,128)(2,1)} %bitcast.10, s32[1024,128]{1,0:T(8,128)} %bitcast.9, bf16[128,128]{1,0:T(8,128)(2,1)} %w_hbm.1, bf16[1024,128]{1,0:T(8,128)(2,1)} %bitcast.11, s32[1,184]{1,0:T(1,128)} %bitcast.12, s32[1,184]{1,0:T(1,128)} %bitcast.13, ...), custom_call_target="tpu_custom_call" | custom-call | tf_op jit(solution)/shard_map/layer/pallas_call | solution.py:492
  66.7 0.0 copy-start
  66.7 0.9 %copy-done = bf16[1024,128]{1,0:T(8,128)(2,1)S(1)} copy-done((bf16[1024,128]{1,0:T(8,128)(2,1)S(1)}, bf16[1024,128]{1,0:T(8,128)(2,1)}, u32[]{:S(2)}) %copy-start) | copy-done | bytes 262168
  67.7 0.0 copy-start.1
  67.7 0.9 %copy-done.1 = bf16[1024,128]{1,0:T(8,128)(2,1)S(1)} copy-done((bf16[1024,128]{1,0:T(8,128)(2,1)S(1)}, bf16[1024,128]{1,0:T(8,128)(2,1)}, u32[]{:S(2)}) %copy-start.1) | copy-done | bytes 262168
  68.6 0.0 copy-start.2
  68.6 0.8 %copy-done.2 = f32[128,128]{1,0:T(8,128)S(1)} copy-done((f32[128,128]{1,0:T(8,128)S(1)}, f32[128,128]{1,0:T(8,128)}, u32[]{:S(2)}) %copy-start.2) | copy-done | bytes 65560
  69.5 0.8 %keep.1 = (bf16[1024,128]{1,0:T(8,128)(2,1)}, f32[128,128]{1,0:T(8,128)}, bf16[1024,128]{1,0:T(8,128)(2,1)}) custom-call(bf16[1024,128]{1,0:T(8,128)(2,1)S(1)} %copy-done, f32[128,128]{1,0:T(8,128)S(1)} %copy-done.2, bf16[1024,128]{1,0:T(8,128)(2,1)S(1)} %copy-done.1), custom_call_target="tpu_custom_call" | custom-call | tf_op jit(solution)/shard_map/keep/pallas_call | solution.py:539
Async XLA Ops:
  66.7 1.0 %copy-start = (bf16[1024,128]{1,0:T(8,128)(2,1)S(1)}, bf16[1024,128]{1,0:T(8,128)(2,1)}, u32[]{:S(2)}) copy-start(bf16[1024,128]{1,0:T(8,128)(2,1)} %get-tuple-element.9.a_ref) | copy-start | bytes 786436
  67.7 0.9 %copy-start.1 = (bf16[1024,128]{1,0:T(8,128)(2,1)S(1)}, bf16[1024,128]{1,0:T(8,128)(2,1)}, u32[]{:S(2)}) copy-start(bf16[1024,128]{1,0:T(8,128)(2,1)} %get-tuple-element.11.c_ref) | copy-start | bytes 786436
  68.6 0.8 %copy-start.2 = (f32[128,128]{1,0:T(8,128)S(1)}, f32[128,128]{1,0:T(8,128)}, u32[]{:S(2)}) copy-start(f32[128,128]{1,0:T(8,128)} %get-tuple-element.10.b_ref) | copy-start | bytes 196612

commit v4 on v3

--- a/solution.py
+++ b/solution.py
@@ -464,13 +464,17 @@
         copy.wait_send()
 
 
-def keep(a_ref, b_ref, c_ref, a_out, b_out, c_out, sem):
-    pairs = ((a_ref, a_out), (b_ref, b_out), (c_ref, c_out))
-    copies = [pltpu.make_async_copy(src, dst, sem.at[i]) for i, (src, dst) in enumerate(pairs)]
-    for copy in copies:
-        copy.start()
-    for copy in copies:
-        copy.wait()
+def keep(a_ref, b_ref, c_ref, a_out, b_out, c_out, a_v, b_v, c_v, sem):
+    triples = ((a_ref, a_v, a_out), (b_ref, b_v, b_out), (c_ref, c_v, c_out))
+    reads = [pltpu.make_async_copy(src, held, sem.at[i]) for i, (src, held, _) in enumerate(triples)]
+    writes = [pltpu.make_async_copy(held, dst, sem.at[3 + i]) for i, (_, held, dst) in enumerate(triples)]
+    for read in reads:
+        read.start()
+    for read, write in zip(reads, writes):
+        read.wait()
+        write.start()
+    for write in writes:
+        write.wait()
 
 
 def body(features, relu_mask, tiles, tile_rows, tile_cols, tile_count, weight, cotangent):
@@ -539,10 +543,10 @@
     out_pre, weight_grad, input_grad = pl.pallas_call(
         keep,
         out_shape=[jax.ShapeDtypeStruct(value.shape, value.dtype) for value in results],
-        in_specs=[in_vmem] * 3,
+        in_specs=[anywhere] * 3,
         out_specs=[anywhere] * 3,
-        scratch_shapes=[pltpu.SemaphoreType.DMA((3,))],
-        compiler_params=pltpu.CompilerParams(vmem_limit_bytes=4 * 1024 * 1024),
+        scratch_shapes=[v(value.shape, value.dtype) for value in results] + [pltpu.SemaphoreType.DMA((6,))],
+        compiler_params=pltpu.CompilerParams(vmem_limit_bytes=67043328),
         name="keep",
     )(*results)
     return out_pre[None], weight_grad, input_grad[None]

time: 71.3 us -> 69.4 us (0.973)
  local copies, waits for them, and re-layouts: 2.73 us -> 0 us
  Pallas kernels: 66.3 us -> 67.1 us
    unnamed x6 -> x0, local copies, waits for them, and re-layouts: 2.73 us -> none
    pallas_call x1, Pallas kernels: 0.83 us -> 1.82 us  [body(): pl.pallas_call(keep, out_shape=[jax.ShapeDtypeStruct(value.shape, value.d...]
where the time goes in v4:
time: 69.4 us; the launch traced here: 68.4 us
  Pallas kernels  67.1 us (97%)
  between operations  1.29 us (2%)
    pallas_call x1, Pallas kernels, body(): pl.pallas_call(functools.partial(kernel, slots, row_blocks, col_blocks, p...  65.3 us
    pallas_call x1, Pallas kernels, body(): pl.pallas_call(keep, out_shape=[jax.ShapeDtypeStruct(value.shape, value.d...  1.82 us

profile of v4, /device:TPU:1, one launch (start us, length us, event | category | flops | bytes accessed | tf_op | source)
XLA Modules:
  0.0 68.4 jit_solution(14249984961493507468)
XLA Ops:
  1.3 65.3 %layer.1 = (bf16[1024,128]{1,0:T(8,128)(2,1)}, f32[128,128]{1,0:T(8,128)}, bf16[1024,128]{1,0:T(8,128)(2,1)}) custom-call(bf16[1024,128]{1,0:T(8,128)(2,1)} %bitcast.10, s32[1024,128]{1,0:T(8,128)} %bitcast.9, bf16[128,128]{1,0:T(8,128)(2,1)} %w_hbm.1, bf16[1024,128]{1,0:T(8,128)(2,1)} %bitcast.11, s32[1,184]{1,0:T(1,128)} %bitcast.12, s32[1,184]{1,0:T(1,128)} %bitcast.13, ...), custom_call_target="tpu_custom_call" | custom-call | tf_op jit(solution)/shard_map/layer/pallas_call | solution.py:496
  66.6 1.8 %keep.1 = (bf16[1024,128]{1,0:T(8,128)(2,1)}, f32[128,128]{1,0:T(8,128)}, bf16[1024,128]{1,0:T(8,128)(2,1)}) custom-call(bf16[1024,128]{1,0:T(8,128)(2,1)} %get-tuple-element.9.a_ref, f32[128,128]{1,0:T(8,128)} %get-tuple-element.10.b_ref, bf16[1024,128]{1,0:T(8,128)(2,1)} %get-tuple-element.11.c_ref), custom_call_target="tpu_custom_call" | custom-call | tf_op jit(solution)/shard_map/keep/pallas_call | solution.py:543
